TPU v7x, 32 devices: a whole 2x2x4 slice. The times are simulated.
32 devices in a mesh: ctx: 8 (over z, y), wsh: 4 (over x, core).
Axes of the slice: x: 2, y: 2, z: 4, core: 2. Of those that a mesh axis runs over, the one named last changes fastest.
Arguments:
- tokens: bfloat16 [4, 1024, 2048], P('wsh', 'ctx'), may hold values from -6 to 6
- out_grad: bfloat16 [4, 1024, 2048], P('wsh', 'ctx'), may hold values from -6 to 6
- attn_weight: bfloat16 [4, 2048, 2048], P(None, None, 'wsh'), may hold values from -0.125 to 0.125
- mlp_weight: bfloat16 [3, 2048, 8192], P(None, None, 'wsh'), may hold values from -0.125 to 0.125
- norm_gains: bfloat16 [4, 2048], P(None, 'wsh'), may hold values from 0.25 to 1.75
- adapt_model: bfloat16 [11, 64, 2048], P(None, None, 'wsh'), may hold values from -0.125 to 0.125
- adapt_hidden: bfloat16 [3, 64, 8192], P(None, None, 'wsh'), may hold values from -0.0625 to 0.0625
- lengths: int32 [4], replicated, may hold values from 512 to 1024, as said below
- adapter_pick: int32 [4], replicated, may hold values from 0 to 3
- block_order: int32 [4, 16], P('wsh'), may hold values from 0 to 15, as said below
Outputs:
- layer_out: bfloat16 [4, 1024, 2048], P('wsh', 'ctx')
- input_grad: float32 [4, 1024, 2048], P('wsh', 'ctx')
- adapt_model_grad: float32 [11, 64, 2048], P(None, None, 'wsh')
- adapt_hidden_grad: float32 [3, 64, 8192], P(None, None, 'wsh')
Inputs may be any that keep to these rules, and one draw needn't show every extreme that they name: `lengths`: some sequence has exactly 1024 valid tokens. Each row of block_order is a permutation of the 16 blocks; the two blocks stored on one index of ctx are p and 15 - p for some p, in either order.
All inputs are finite; a program needn't handle non-finite values.
Results may differ from a plain program's by a relative error of at most 0.017.
Values may be sent and summed in bfloat16 or wider, within the bound.
No kernel may reach another device: no remote copies, remote signals or barrier semaphores. Data moves between devices by JAX's collectives and lax.ppermute only.
A program may use at most 512 MiB of HBM per device.

v0:
```python
import jax
import jax.numpy as jnp
from jax import lax
from jax.sharding import PartitionSpec as P

HEADS = 16
HEAD_DIM = 128
FF = 8192
RANK = 16
ADAPTERS = 4
NORM_EPS = 1e-06
ADAPTER_SCALE = 4.0
ROPE_BASE = 500000.0


def rms_scale(values):
    return lax.rsqrt(jnp.mean(values * values, axis=-1, keepdims=True) + NORM_EPS)


def norm_back(values, scale_rows, upstream):
    return scale_rows * upstream - values * scale_rows**3 * jnp.mean(
        upstream * values, axis=-1, keepdims=True
    )


def rotary_tables(positions, head_dim):
    half_dim = head_dim // 2
    frequency = ROPE_BASE ** (-(jnp.arange(half_dim, dtype=jnp.float32) * 2.0) / head_dim)
    angles = positions.astype(jnp.float32)[:, None] * frequency[None, :]
    return (jnp.cos(angles)[:, None, :], jnp.sin(angles)[:, None, :])


def rotate(values, tables, heads_total):
    cosine, sine_part = tables
    row_count = values.shape[0]
    shaped = values.reshape(row_count, heads_total, -1)
    half_dim = shaped.shape[-1] // 2
    first_half = shaped[..., :half_dim]
    second_half = shaped[..., half_dim:]
    turned = jnp.concatenate(
        [
            first_half * cosine - second_half * sine_part,
            second_half * cosine + first_half * sine_part,
        ],
        axis=-1,
    )
    return turned.reshape(row_count, -1)


def rotate_back(gradient, tables, heads_total):
    cosine, sine_part = tables
    row_count = gradient.shape[0]
    shaped = gradient.reshape(row_count, heads_total, -1)
    half_dim = shaped.shape[-1] // 2
    first_half = shaped[..., :half_dim]
    second_half = shaped[..., half_dim:]
    turned = jnp.concatenate(
        [
            first_half * cosine + second_half * sine_part,
            second_half * cosine - first_half * sine_part,
        ],
        axis=-1,
    )
    return turned.reshape(row_count, -1)


def pick_rows(stacked, onehot, adapters):
    part_count, col_count = (stacked.shape[0], stacked.shape[2])
    split_view = stacked.reshape(part_count, adapters, -1, col_count)
    return jnp.einsum(
        "kard,a->krd", split_view, onehot.astype(stacked.dtype), preferred_element_type=jnp.float32
    ).astype(stacked.dtype)


def per_device(
    tokens,
    out_grad,
    attn_weight,
    mlp_weight,
    norm_gains,
    adapt_model,
    adapt_hidden,
    lengths,
    adapter_pick,
    block_order,
):
    input_rows = tokens[0]
    row_count, model_dim = input_rows.shape
    block_rows = row_count // 2
    ctx_size = lax.axis_size("ctx")
    slot_rows = row_count * ctx_size
    heads_all = HEADS
    head_dim = HEAD_DIM
    adapters = ADAPTERS
    score_scale = head_dim ** (-0.5)
    seq_index = lax.axis_index("wsh")
    ctx_index = lax.axis_index("ctx")
    seq_length = lax.dynamic_index_in_dim(lengths, seq_index, keepdims=False)
    chosen = lax.dynamic_index_in_dim(adapter_pick, seq_index, keepdims=False)
    onehot = (jnp.arange(adapters) == chosen).astype(jnp.float32)
    all_positions = (
        block_order[0][:, None] * block_rows + jnp.arange(block_rows)[None, :]
    ).reshape(-1)
    own_positions = lax.dynamic_slice_in_dim(all_positions, ctx_index * row_count, row_count)
    valid_rows = (own_positions < seq_length).astype(jnp.float32)[:, None]
    tables = rotary_tables(own_positions, head_dim)
    key_allowed = (all_positions[None, :] <= own_positions[:, None]) & (
        all_positions[None, :] < seq_length
    )

    def heads_view(matrix):
        return matrix.reshape(matrix.shape[0], heads_all, head_dim)

    attn_full, gains_full, adapt_full = (
        lax.all_gather(attn_weight, "wsh", axis=2, tiled=True),
        lax.all_gather(norm_gains, "wsh", axis=1, tiled=True),
        lax.all_gather(adapt_model, "wsh", axis=2, tiled=True),
    )
    gain_rows = gains_full.astype(jnp.float32)
    model_reduced = pick_rows(adapt_full, onehot, adapters)
    projected_rows = jnp.einsum(
        "td,kde->kte", input_rows, attn_full[:3], preferred_element_type=jnp.float32
    )
    low_in = jnp.einsum(
        "td,krd->ktr", input_rows, model_reduced[:3], preferred_element_type=jnp.float32
    ).astype(jnp.bfloat16)
    projected_rows = projected_rows + ADAPTER_SCALE * jnp.einsum(
        "ktr,krd->ktd", low_in, model_reduced[6:9], preferred_element_type=jnp.float32
    )
    query_scale = rms_scale(projected_rows[0])
    key_scale = rms_scale(projected_rows[1])
    queries = rotate(projected_rows[0] * query_scale * gain_rows[0], tables, heads_all).astype(
        jnp.bfloat16
    )
    own_keys = rotate(projected_rows[1] * key_scale * gain_rows[1], tables, heads_all).astype(
        jnp.bfloat16
    )
    own_values = projected_rows[2].astype(jnp.bfloat16)
    all_keys, all_values = (
        lax.all_gather(own_keys, "ctx", axis=0, tiled=True),
        lax.all_gather(own_values, "ctx", axis=0, tiled=True),
    )
    query_heads = heads_view(queries)
    key_heads = heads_view(all_keys)
    value_heads = heads_view(all_values)
    scores = (
        jnp.einsum("thd,shd->hts", query_heads, key_heads, preferred_element_type=jnp.float32)
        * score_scale
    )
    scores = jnp.where(key_allowed[None], scores, -jnp.inf)
    row_max = jnp.max(scores, axis=-1, keepdims=True)
    log_full = row_max + jnp.log(jnp.sum(jnp.exp(scores - row_max), axis=-1, keepdims=True))
    weights = jnp.exp(scores - log_full).astype(jnp.bfloat16)
    attended = (
        jnp.einsum("hts,shd->thd", weights, value_heads, preferred_element_type=jnp.float32)
        .reshape(row_count, model_dim)
        .astype(jnp.bfloat16)
    )
    log_totals = log_full[..., 0]
    reduced_output = jnp.einsum(
        "td,rd->tr", attended, model_reduced[3], preferred_element_type=jnp.float32
    ).astype(jnp.bfloat16)
    branch = jnp.dot(
        attended, attn_full[3], preferred_element_type=jnp.float32
    ) + ADAPTER_SCALE * jnp.dot(
        reduced_output, model_reduced[9], preferred_element_type=jnp.float32
    )
    branch_scale = rms_scale(branch)
    hidden_in = input_rows.astype(jnp.float32) + branch * branch_scale * gain_rows[2]
    hidden_low = hidden_in.astype(jnp.bfloat16)
    reduced_gate_up = jnp.einsum(
        "td,krd->ktr", hidden_low, model_reduced[4:6], preferred_element_type=jnp.float32
    ).astype(jnp.bfloat16)

    def gate_up_parts(weight_piece, gathered_rows):
        gate_part = jnp.dot(
            hidden_low, weight_piece[0], preferred_element_type=jnp.float32
        ) + ADAPTER_SCALE * jnp.dot(
            reduced_gate_up[0], gathered_rows[0], preferred_element_type=jnp.float32
        )
        up_part = jnp.dot(
            hidden_low, weight_piece[1], preferred_element_type=jnp.float32
        ) + ADAPTER_SCALE * jnp.dot(
            reduced_gate_up[1], gathered_rows[1], preferred_element_type=jnp.float32
        )
        return (gate_part, up_part)

    weight_piece = lax.all_gather(mlp_weight, "wsh", axis=2, tiled=True)
    adapt_piece = lax.all_gather(adapt_hidden, "wsh", axis=2, tiled=True)
    gathered_rows = pick_rows(adapt_piece, onehot, adapters)
    gate_part, up_part = gate_up_parts(weight_piece, gathered_rows)
    product = (jax.nn.silu(gate_part) * up_part).astype(jnp.bfloat16)
    down_total_sum = jnp.einsum(
        "tn,dn->td", product, weight_piece[2], preferred_element_type=jnp.float32
    )
    low_down_sum = jnp.einsum(
        "tn,rn->tr", product, gathered_rows[2], preferred_element_type=jnp.float32
    )
    down_total_sum, low_down_sum = (down_total_sum, low_down_sum)
    low_down = low_down_sum.astype(jnp.bfloat16)
    feedforward_output = down_total_sum + ADAPTER_SCALE * jnp.dot(
        low_down, model_reduced[10], preferred_element_type=jnp.float32
    )
    mlp_scale = rms_scale(feedforward_output)
    result = hidden_in + feedforward_output * mlp_scale * gain_rows[3]
    upstream = out_grad[0].astype(jnp.float32) * valid_rows
    grad_mlp_out = norm_back(feedforward_output, mlp_scale, upstream * gain_rows[3]).astype(
        jnp.bfloat16
    )
    grad_low_down = (
        ADAPTER_SCALE
        * jnp.einsum(
            "td,rd->tr", grad_mlp_out, model_reduced[10], preferred_element_type=jnp.float32
        )
    ).astype(jnp.bfloat16)
    gradient_down_factor = ADAPTER_SCALE * jnp.einsum(
        "tr,td->rd", low_down, grad_mlp_out, preferred_element_type=jnp.float32
    )
    weight_piece = lax.all_gather(mlp_weight, "wsh", axis=2, tiled=True)
    adapt_piece = lax.all_gather(adapt_hidden, "wsh", axis=2, tiled=True)
    gathered_rows = pick_rows(adapt_piece, onehot, adapters)
    gate_part, up_part = gate_up_parts(weight_piece, gathered_rows)
    sigmoid_gate = jax.nn.sigmoid(gate_part)
    silu_gate = gate_part * sigmoid_gate
    product = (silu_gate * up_part).astype(jnp.bfloat16)
    grad_product = jnp.dot(
        grad_mlp_out, weight_piece[2], preferred_element_type=jnp.float32
    ) + jnp.dot(grad_low_down, gathered_rows[2], preferred_element_type=jnp.float32)
    grad_gate = (
        grad_product * up_part * sigmoid_gate * (1.0 + gate_part * (1.0 - sigmoid_gate))
    ).astype(jnp.bfloat16)
    grad_up = (grad_product * silu_gate).astype(jnp.bfloat16)
    input_sum = jnp.einsum(
        "tn,dn->td", grad_gate, weight_piece[0], preferred_element_type=jnp.float32
    ) + jnp.einsum("tn,dn->td", grad_up, weight_piece[1], preferred_element_type=jnp.float32)
    reduced_sum = ADAPTER_SCALE * jnp.stack(
        [
            jnp.einsum(
                "tn,rn->tr", grad_gate, gathered_rows[0], preferred_element_type=jnp.float32
            ),
            jnp.einsum("tn,rn->tr", grad_up, gathered_rows[1], preferred_element_type=jnp.float32),
        ]
    )
    piece_grads = jnp.stack(
        [
            ADAPTER_SCALE
            * jnp.einsum(
                "tr,tn->rn", reduced_gate_up[0], grad_gate, preferred_element_type=jnp.float32
            ),
            ADAPTER_SCALE
            * jnp.einsum(
                "tr,tn->rn", reduced_gate_up[1], grad_up, preferred_element_type=jnp.float32
            ),
            jnp.einsum("tr,tn->rn", grad_low_down, product, preferred_element_type=jnp.float32),
        ]
    )
    input_sum, reduced_sum, picked_hidden = (input_sum, reduced_sum, piece_grads)
    low_grads = reduced_sum.astype(jnp.bfloat16)
    grad_hidden = (
        upstream
        + input_sum
        + jnp.einsum(
            "ktr,krd->td", low_grads, model_reduced[4:6], preferred_element_type=jnp.float32
        )
    )
    grad_a_gate_up = jnp.einsum(
        "ktr,td->krd", low_grads, hidden_low, preferred_element_type=jnp.float32
    )
    grad_branch = norm_back(branch, branch_scale, grad_hidden * gain_rows[2]).astype(jnp.bfloat16)
    grad_low_out = (
        ADAPTER_SCALE
        * jnp.einsum("td,rd->tr", grad_branch, model_reduced[9], preferred_element_type=jnp.float32)
    ).astype(jnp.bfloat16)
    gradient_output_factor = ADAPTER_SCALE * jnp.einsum(
        "tr,td->rd", reduced_output, grad_branch, preferred_element_type=jnp.float32
    )
    grad_a_out = jnp.einsum("tr,td->rd", grad_low_out, attended, preferred_element_type=jnp.float32)
    grad_attended = (
        jnp.einsum("te,de->td", grad_branch, attn_full[3], preferred_element_type=jnp.float32)
        + jnp.einsum(
            "tr,rd->td", grad_low_out, model_reduced[3], preferred_element_type=jnp.float32
        )
    ).astype(jnp.bfloat16)
    grad_heads = heads_view(grad_attended)
    scores = (
        jnp.einsum("thd,shd->hts", query_heads, key_heads, preferred_element_type=jnp.float32)
        * score_scale
    )
    scores = jnp.where(key_allowed[None], scores, -jnp.inf)
    weights_full = jnp.exp(scores - log_totals[..., None])
    grad_probs = jnp.einsum(
        "thd,shd->hts", grad_heads, value_heads, preferred_element_type=jnp.float32
    )
    row_delta = jnp.sum(weights_full * grad_probs, axis=-1, keepdims=True)
    grad_scores = (weights_full * (grad_probs - row_delta)).astype(jnp.bfloat16)
    grad_queries = (
        jnp.einsum("hts,shd->thd", grad_scores, key_heads, preferred_element_type=jnp.float32)
        * score_scale
    ).reshape(row_count, model_dim)
    key_full = (
        jnp.einsum("hts,thd->shd", grad_scores, query_heads, preferred_element_type=jnp.float32)
        * score_scale
    ).reshape(slot_rows, model_dim)
    value_full = jnp.einsum(
        "hts,thd->shd",
        weights_full.astype(jnp.bfloat16),
        grad_heads,
        preferred_element_type=jnp.float32,
    ).reshape(slot_rows, model_dim)
    grad_keys, grad_values = (
        lax.psum_scatter(key_full, "ctx", scatter_dimension=0, tiled=True),
        lax.psum_scatter(value_full, "ctx", scatter_dimension=0, tiled=True),
    )
    grad_proj_query = norm_back(
        projected_rows[0], query_scale, rotate_back(grad_queries, tables, heads_all) * gain_rows[0]
    ).astype(jnp.bfloat16)
    grad_proj_key = norm_back(
        projected_rows[1], key_scale, rotate_back(grad_keys, tables, heads_all) * gain_rows[1]
    ).astype(jnp.bfloat16)
    grad_proj = jnp.stack([grad_proj_query, grad_proj_key, grad_values.astype(jnp.bfloat16)])
    grad_low_qkv = (
        ADAPTER_SCALE
        * jnp.einsum(
            "ktd,krd->ktr", grad_proj, model_reduced[6:9], preferred_element_type=jnp.float32
        )
    ).astype(jnp.bfloat16)
    gradient_projection_factor = ADAPTER_SCALE * jnp.einsum(
        "ktr,ktd->krd", low_in, grad_proj, preferred_element_type=jnp.float32
    )
    grad_a_qkv = jnp.einsum(
        "ktr,td->krd", grad_low_qkv, input_rows, preferred_element_type=jnp.float32
    )
    grad_inputs = (
        grad_hidden
        + jnp.einsum("kte,kde->td", grad_proj, attn_full[:3], preferred_element_type=jnp.float32)
        + jnp.einsum(
            "ktr,krd->td", grad_low_qkv, model_reduced[:3], preferred_element_type=jnp.float32
        )
    )
    picked_model = jnp.concatenate(
        [
            grad_a_qkv,
            grad_a_out[None],
            grad_a_gate_up,
            gradient_projection_factor,
            gradient_output_factor[None],
            gradient_down_factor[None],
        ],
        axis=0,
    )
    spread_model = (onehot[None, :, None, None] * picked_model[:, None]).reshape(
        picked_model.shape[0], adapters * RANK, model_dim
    )
    spread_hidden = (onehot[None, :, None, None] * picked_hidden[:, None]).reshape(
        picked_hidden.shape[0], adapters * RANK, FF
    )
    shard_model, shard_hidden = (
        lax.psum_scatter(spread_model, "wsh", scatter_dimension=2, tiled=True),
        lax.psum_scatter(spread_hidden, "wsh", scatter_dimension=2, tiled=True),
    )
    model_grads, hidden_grads_out = lax.psum((shard_model, shard_hidden), "ctx")
    return (result.astype(jnp.bfloat16)[None], grad_inputs[None], model_grads, hidden_grads_out)


def solution(mesh):
    in_specs = (
        P("wsh", "ctx", None),
        P("wsh", "ctx", None),
        P(None, None, "wsh"),
        P(None, None, "wsh"),
        P(None, "wsh"),
        P(None, None, "wsh"),
        P(None, None, "wsh"),
        P(),
        P(),
        P("wsh", None),
    )
    out_specs = (
        P("wsh", "ctx", None),
        P("wsh", "ctx", None),
        P(None, None, "wsh"),
        P(None, None, "wsh"),
    )
    return jax.shard_map(
        per_device, mesh=mesh, in_specs=in_specs, out_specs=out_specs, check_vma=False
    )
```

profile of v0, /device:TPU:0, one launch (start us, length us, event | category | flops | bytes accessed | tf_op | source)
XLA Modules:
  0.0 1708.9 jit_solution(13489928325962978200)
XLA Ops:
  7.9 11.5 copy.32
  20.4 6.4 all_gather.26
  29.2 10.2 all-gather.10.cloned.1.call-done
  39.4 4.8 fusion.19
  45.8 196.8 %all-gather.8.cloned.1.call-done = bf16[4,2048,2048]{1,2,0:T(8,128)(2,1)} async-done(((bf16[4,2048,512]{1,2,0:T(8,128)(2,1)}), bf16[4,2048,2048]{1,2,0:T(8,128)(2,1)}) %all-gather.8.cloned.1.call-update) | async-done | bytes 33554448 | tf_op jit(solution)/shard_map/all_gather | solution.py:115
  242.6 11.9 fusion.74
  257.7 2.8 copy.34
  260.4 2.5 copy.35
  268.2 2.1 copy.36
  272.9 6.7 fusion.17
  281.4 67.9 %all-gather.12.cloned.1.call-done = bf16[1024,2048]{0,1:T(8,128)(2,1)} async-done(((bf16[128,2048]{0,1:T(8,128)(2,1)}), bf16[1024,2048]{0,1:T(8,128)(2,1)}) %all-gather.12.cloned.1.call-update) | async-done | bytes 4194320 | tf_op jit(solution)/shard_map/all_gather | solution.py:140
  349.3 4.3 fusion.14
  353.6 2.5 exponential_reduce_fusion
  356.9 67.7 %all-gather.18.cloned.1.call-done = bf16[1,1024,2048]{1,2,0:T(8,128)(2,1)} async-done(((bf16[1,128,2048]{1,2,0:T(8,128)(2,1)}), bf16[1,1024,2048]{1,2,0:T(8,128)(2,1)}) %all-gather.18.cloned.1.call-update) | async-done | bytes 4194320 | tf_op jit(solution)/shard_map/all_gather | solution.py:141
  424.6 7.2 convolution_convert_fusion
  432.0 9.3 fusion.13
  442.3 565.8 %all-gather.14.cloned.1.call-done = bf16[3,2048,8192]{2,1,0:T(8,128)(2,1)} async-done(((bf16[3,2048,2048]{2,1,0:T(8,128)(2,1)}), bf16[3,2048,8192]{2,1,0:T(8,128)(2,1)}) %all-gather.14.cloned.1.call-update) | async-done | bytes 100663312 | tf_op jit(solution)/shard_map/all_gather | solution.py:188
  1008.1 15.0 fusion.1
  1023.1 5.0 fusion.8
  1028.1 15.2 fusion.3
  1043.3 7.1 multiply_convert_fusion.3
  1052.2 15.8 fusion.5
  1070.0 15.2 fusion.4
  1085.2 7.1 multiply_convert_fusion.1
  1093.6 16.7 fusion
  1110.4 17.0 fusion.37
  1130.7 4.6 fusion.12
  1136.0 8.2 multiply_reduce_fusion
  1144.2 2.6 multiply_convert_fusion
  1146.8 4.7 broadcast_multiply_fusion
  1151.6 9.4 fusion.81
  1163.0 2.2 fusion.10
  1165.7 3.4 bitcast_multiply_fusion
  1169.1 4.8 fusion.45
  1173.9 125.7 %reduce-scatter.5.cloned.1.call-done = f32[128,2048]{0,1:T(8,128)} async-done(((f32[1024,2048]{0,1:T(8,128)}), f32[128,2048]{0,1:T(8,128)}) %reduce-scatter.5.cloned.1.call-update) | async-done | bytes 1048592 | tf_op jit(solution)/shard_map/reduce_scatter | solution.py:311
  1299.6 2.1 fusion.98
  1306.7 2.7 copy.41
  1309.4 3.0 pad_maximum_fusion.3
  1312.4 2.5 copy.46
  1316.9 133.3 %reduce-scatter.7.cloned.1.call-done = f32[128,2048]{0,1:T(8,128)} async-done(((f32[1024,2048]{0,1:T(8,128)}), f32[128,2048]{0,1:T(8,128)}) %reduce-scatter.7.cloned.1.call-update) | async-done | bytes 1048592 | tf_op jit(solution)/shard_map/reduce_scatter | solution.py:312
  1451.5 2.1 fusion.65
  1457.0 3.3 bitcast_multiply_fusion.1
  1460.4 49.5 %reduce-scatter.11.cloned.1.call-done = f32[3,64,2048]{2,1,0:T(8,128)} async-done(((f32[3,64,8192]{2,1,0:T(8,128)}), f32[3,64,2048]{2,1,0:T(8,128)}) %reduce-scatter.11.cloned.1.call-update) | async-done | bytes 1572880 | tf_op jit(solution)/shard_map/reduce_scatter | solution.py:359
  1509.8 57.0 %reduce-scatter.9.cloned.1.call-done = f32[11,64,512]{2,1,0:T(8,128)} async-done(((f32[11,64,2048]{2,1,0:T(8,128)}), f32[11,64,512]{2,1,0:T(8,128)}) %reduce-scatter.9.cloned.1.call-update) | async-done | bytes 1441808 | tf_op jit(solution)/shard_map/reduce_scatter | solution.py:358
  1568.1 11.3 fusion.32
  1579.4 117.3 %all-reduce.3.cloned.1.call-done = (f32[11,64,512]{2,1,0:T(8,128)}, f32[3,64,2048]{2,1,0:T(8,128)}) async-done(((f32[11,64,512]{2,1,0:T(8,128)}, f32[3,64,2048]{2,1,0:T(8,128)}), (f32[11,64,512]{2,1,0:T(8,128)}, f32[3,64,2048]{2,1,0:T(8,128)})) %all-reduce.3.cloned.1.call-update) | async-done | bytes 3014672 | tf_op jit(solution)/shard_map/psum | solution.py:361
  1696.7 2.6 copy.86
  1699.3 2.7 copy.87
  (214 shorter events, 44.5 us)
Async XLA Ops:
  7.2 32.2 %all-gather.10.cloned.1.call-start = ((), (), s32[]{:S(2)}) async-start(), calls=%async_computation.5 | async-start | bytes 3604480 | tf_op jit(solution)/shard_map/all_gather | solution.py:117
  7.9 234.7 %all-gather.8.cloned.1.call-start = ((), (), s32[]{:S(2)}) async-start(), calls=%async_computation.4 | async-start | bytes 41943040 | tf_op jit(solution)/shard_map/all_gather | solution.py:115
  19.5 7.4 copy-start.58
  19.5 8.8 copy-start.59
  19.5 253.4 %all-gather.16.cloned.1.call-start = ((), (), s32[]{:S(2)}) async-start(), calls=%async_computation.8 | async-start | bytes 3932160 | tf_op jit(solution)/shard_map/all_gather | solution.py:189
  20.2 329.1 %all-gather.12.cloned.1.call-start = ((), (), s32[]{:S(2)}) async-start(), calls=%async_computation.6 | async-start | bytes 4718592 | tf_op jit(solution)/shard_map/all_gather | solution.py:140
  26.9 236.9 %copy-start.42 = (f32[1,2048]{1,0:T(1,128)}, f32[1,2048]{1,0:T(1,128)S(1)}, u32[]{:S(2)}) copy-start(f32[1,2048]{1,0:T(1,128)S(1)} %get-tuple-element.38) | copy-start | bytes 24580
  26.9 238.3 %copy-start.44 = (f32[1,2048]{1,0:T(1,128)}, f32[1,2048]{1,0:T(1,128)S(1)}, u32[]{:S(2)}) copy-start(f32[1,2048]{1,0:T(1,128)S(1)} %get-tuple-element.39) | copy-start | bytes 24580
  29.1 236.3 %copy-start.32 = (f32[128,64]{1,0:T(8,128)}, f32[128,64]{1,0:T(8,128)S(1)}, u32[]{:S(2)}) copy-start(f32[128,64]{1,0:T(8,128)S(1)} %get-tuple-element.40) | copy-start | bytes 98308
  29.1 236.3 %copy-start.34 = (f32[128,64]{1,0:T(8,128)}, f32[128,64]{1,0:T(8,128)S(1)}, u32[]{:S(2)}) copy-start(f32[128,64]{1,0:T(8,128)S(1)} %get-tuple-element.41) | copy-start | bytes 98308
  39.4 6.1 copy-start.4
  45.8 208.7 %copy-start.46 = (bf16[3,16,128]{2,1,0:T(8,128)(2,1)}, bf16[3,16,128]{2,1,0:T(8,128)(2,1)S(1)}, u32[]{:S(2)}) copy-start(bf16[3,16,128]{2,1,0:T(8,128)(2,1)S(1)} %convolution_convert_fusion.1) | copy-start | bytes 36868
  256.1 14.3 copy-start.1
  270.3 154.3 %all-gather.18.cloned.1.call-start = ((), (), s32[]{:S(2)}) async-start(), calls=%async_computation.13 | async-start | bytes 4718592 | tf_op jit(solution)/shard_map/all_gather | solution.py:141
  271.3 736.9 %all-gather.14.cloned.1.call-start = ((), (), s32[]{:S(2)}) async-start(), calls=%async_computation.7 | async-start | bytes 125829120 | tf_op jit(solution)/shard_map/all_gather | solution.py:188
  271.8 1027.7 %reduce-scatter.5.cloned.1.call-start = ((), (), s32[]{:S(2)}) async-start(), calls=%async_computation.9 | async-start | bytes 9437184 | tf_op jit(solution)/shard_map/reduce_scatter | solution.py:311
  272.9 76.4 %copy-start.20 = (bf16[128,16,64]{2,0,1:T(8,128)(2,1)S(1)}, bf16[128,16,64]{2,0,1:T(8,128)(2,1)}, u32[]{:S(2)}) copy-start(bf16[128,16,64]{2,0,1:T(8,128)(2,1)} %get-tuple-element.24) | copy-start | bytes 786436
  272.9 76.4 %copy-start.22 = (bf16[128,16,64]{2,0,1:T(8,128)(2,1)S(1)}, bf16[128,16,64]{2,0,1:T(8,128)(2,1)}, u32[]{:S(2)}) copy-start(bf16[128,16,64]{2,0,1:T(8,128)(2,1)} %get-tuple-element.25) | copy-start | bytes 786436
  424.6 7.2 copy-start.13
  431.8 9.6 copy-start.28
  432.0 9.4 copy-start.48
  432.0 9.8 copy-start.5
  442.1 586.1 %copy-start.14 = (bf16[128,2048]{1,0:T(8,128)(2,1)}, bf16[128,2048]{1,0:T(8,128)(2,1)S(1)}, u32[]{:S(2)}) copy-start(bf16[128,2048]{1,0:T(8,128)(2,1)S(1)} %fusion.68) | copy-start | bytes 1572868
  1050.5 17.5 %copy-start.7 = (bf16[128,8192]{1,0:T(8,128)(2,1)}, bf16[128,8192]{1,0:T(8,128)(2,1)S(1)}, u32[]{:S(2)}) copy-start(bf16[128,8192]{1,0:T(8,128)(2,1)S(1)} %get-tuple-element.54) | copy-start | bytes 6291460
  1052.2 15.8 copy-start.30
  1085.2 7.1 copy-start.24
  1092.3 18.1 %copy-start.11 = (bf16[128,8192]{1,0:T(8,128)(2,1)}, bf16[128,8192]{1,0:T(8,128)(2,1)S(1)}, u32[]{:S(2)}) copy-start(bf16[128,8192]{1,0:T(8,128)(2,1)S(1)} %get-tuple-element.14) | copy-start | bytes 6291460
  1093.6 16.8 copy-start.31
  1130.4 4.9 copy-start.18
  1136.0 8.2 slice-start
  1136.0 8.2 slice-start.1
  1151.6 298.6 %reduce-scatter.7.cloned.1.call-start = ((), (), s32[]{:S(2)}) async-start(), calls=%async_computation.10 | async-start | bytes 9437184 | tf_op jit(solution)/shard_map/reduce_scatter | solution.py:312
  1161.0 348.8 %reduce-scatter.11.cloned.1.call-start = ((), (), s32[]{:S(2)}) async-start(), calls=%async_computation.12 | async-start | bytes 7864320 | tf_op jit(solution)/shard_map/reduce_scatter | solution.py:359
  1169.1 397.7 %reduce-scatter.9.cloned.1.call-start = ((), (), s32[]{:S(2)}) async-start(), calls=%async_computation.11 | async-start | bytes 7208960 | tf_op jit(solution)/shard_map/reduce_scatter | solution.py:358
  1173.9 129.5 %copy-start.33 = (f32[128,64]{1,0:T(8,128)S(1)}, f32[128,64]{1,0:T(8,128)}, u32[]{:S(2)}) copy-start(f32[128,64]{1,0:T(8,128)} %copy-done.32) | copy-start | bytes 98308
  1173.9 129.5 %copy-start.35 = (f32[128,64]{1,0:T(8,128)S(1)}, f32[128,64]{1,0:T(8,128)}, u32[]{:S(2)}) copy-start(f32[128,64]{1,0:T(8,128)} %copy-done.34) | copy-start | bytes 98308
  1306.7 8.2 copy-start.2
  1306.7 8.2 copy-start.43
  1306.7 8.2 copy-start.45
  1312.4 139.1 %copy-start.51 = (f32[128]{0:T(128)S(1)}, f32[128]{0:T(128)}, u32[]{:S(2)}) copy-start(f32[128]{0:T(128)} %copy-done.50) | copy-start | bytes 1540
  1312.4 139.1 %copy-start.53 = (f32[128]{0:T(128)S(1)}, f32[128]{0:T(128)}, u32[]{:S(2)}) copy-start(f32[128]{0:T(128)} %copy-done.52) | copy-start | bytes 1540
  1312.4 139.1 %copy-start.55 = (f32[128]{0:T(128)S(1)}, f32[128]{0:T(128)}, u32[]{:S(2)}) copy-start(f32[128]{0:T(128)} %get-tuple-element.44) | copy-start | bytes 1540
  1312.4 139.1 %copy-start.56 = (f32[128]{0:T(128)S(1)}, f32[128]{0:T(128)}, u32[]{:S(2)}) copy-start(f32[128]{0:T(128)} %get-tuple-element.62) | copy-start | bytes 1540
  1460.3 107.8 %copy-start.27 = (f32[128,2048]{1,0:T(8,128)S(1)}, f32[128,2048]{1,0:T(8,128)}, u32[]{:S(2)}) copy-start(f32[128,2048]{1,0:T(8,128)} %copy-done.26) | copy-start | bytes 3145732
  1460.3 107.8 %copy-start.37 = (bf16[1,128,2048]{1,2,0:T(8,128)(2,1)S(1)}, bf16[1,128,2048]{1,2,0:T(8,128)(2,1)}, u32[]{:S(2)}) copy-start(bf16[1,128,2048]{1,2,0:T(8,128)(2,1)} %copy-done.36) | copy-start | bytes 1572868
  1460.3 107.8 %copy-start.39 = (bf16[1,128,2048]{1,2,0:T(8,128)(2,1)S(1)}, bf16[1,128,2048]{1,2,0:T(8,128)(2,1)}, u32[]{:S(2)}) copy-start(bf16[1,128,2048]{1,2,0:T(8,128)(2,1)} %copy-done.38) | copy-start | bytes 1572868
  1460.3 107.8 %copy-start.41 = (bf16[1,128,2048]{1,2,0:T(8,128)(2,1)S(1)}, bf16[1,128,2048]{1,2,0:T(8,128)(2,1)}, u32[]{:S(2)}) copy-start(bf16[1,128,2048]{1,2,0:T(8,128)(2,1)} %copy-done.40) | copy-start | bytes 1572868
  1460.3 236.4 %all-reduce.3.cloned.1.call-start = ((), (), s32[]{:S(2)}) async-start(), calls=%async_computation.14 | async-start | bytes 6029312 | tf_op jit(solution)/shard_map/psum | solution.py:361
  (25 other events, 65.0 us)
Sparse Core Ops, SparseCore 0:
  9.5 29.8 all-gather.9
  41.0 201.5 all-gather.7
  244.1 28.4 all-gather.15
  274.6 74.6 all-gather.11
  351.8 72.8 all-gather.17
  426.0 582.0 all-gather.13
  1151.7 147.8 reduce-scatter.4
  1303.2 146.9 reduce-scatter.6
  1452.7 57.0 reduce-scatter.10
  1512.2 54.5 reduce-scatter.8
  1570.6 126.0 all-reduce.2
where the time goes:
time: 1720 us; the launch traced here: 1710 us
  waiting for transfers between devices  1390 us (81%)
  matrix products  217 us (13%)
  local copies, waits for them, and re-layouts  42.7 us (2%)
  other arithmetic  33.2 us (2%)
    all_gather x1, waiting for transfers between devices, per_device(): weight_piece = lax.all_gather(mlp_weight, 'wsh', axis=2, tiled=True)  566 us
    all_gather x1, waiting for transfers between devices, per_device(): lax.all_gather(attn_weight, 'wsh', axis=2, tiled=True)  197 us
    reduce_scatter x1, waiting for transfers between devices, per_device(): lax.psum_scatter(value_full, 'ctx', scatter_dimension=0, tiled=True)  133 us
    reduce_scatter x1, waiting for transfers between devices, per_device(): lax.psum_scatter(key_full, 'ctx', scatter_dimension=0, tiled=True)  126 us
    psum x1, waiting for transfers between devices, per_device(): model_grads, hidden_grads_out = lax.psum((shard_model, shard_hidden), 'ctx')  117 us
    all_gather x1, waiting for transfers between devices, per_device(): lax.all_gather(own_keys, 'ctx', axis=0, tiled=True)  67.9 us
    all_gather x1, waiting for transfers between devices, per_device(): lax.all_gather(own_values, 'ctx', axis=0, tiled=True)  67.7 us
    reduce_scatter x1, waiting for transfers between devices, per_device(): lax.psum_scatter(spread_model, 'wsh', scatter_dimension=2, tiled=True)  57 us
  transfers between devices with their start and end apart: 11, of which 10 were waited for; matrix products, arithmetic and copies ran while one was open for 8% of the time, Pallas kernels for 0%

commit v1 on v0

--- a/solution.py
+++ b/solution.py
@@ -2,6 +2,7 @@
 import jax.numpy as jnp
 from jax import lax
 from jax.sharding import PartitionSpec as P
+from jax.lax import axis_index, axis_size, ppermute
 
 HEADS = 16
 HEAD_DIM = 128
@@ -185,7 +186,14 @@
         )
         return (gate_part, up_part)
 
-    weight_piece = lax.all_gather(mlp_weight, "wsh", axis=2, tiled=True)
+    a_next, carry = (axis_size("wsh"), axis_index("wsh"))
+    weight_piece, mixed_arr = (mlp_weight, 1)
+    while mixed_arr < a_next:
+        t_next = ppermute(weight_piece, "wsh", [(nth, nth ^ mixed_arr) for nth in range(a_next)])
+        after = jnp.concatenate([weight_piece, t_next], 2)
+        piece_now = jnp.concatenate([t_next, weight_piece], 2)
+        weight_piece = jnp.where(carry & mixed_arr == 0, after, piece_now)
+        mixed_arr = 2 * mixed_arr
     adapt_piece = lax.all_gather(adapt_hidden, "wsh", axis=2, tiled=True)
     gathered_rows = pick_rows(adapt_piece, onehot, adapters)
     gate_part, up_part = gate_up_parts(weight_piece, gathered_rows)

time: 1720 us -> 2810 us (1.63)
  waiting for transfers between devices: 1390 us -> 2300 us
  other arithmetic: 33.2 us -> 181 us
  matrix products: 217 us -> 253 us
    ppermute x0 -> x2, waiting for transfers between devices: none -> 1570 us  [per_device(): ppermute(weight_piece, 'wsh', [(nth, nth ^ mixed_arr) for nth in range(a_...]
    all_gather x1, waiting for transfers between devices: 566 us -> 0.01 us  [per_device(): weight_piece = lax.all_gather(mlp_weight, 'wsh', axis=2, tiled=True)]
    select_n x0 -> x2, other arithmetic: none -> 146 us  [per_device(): weight_piece = jnp.where(carry & mixed_arr == 0, after, piece_now)]
    all_gather x1, waiting for transfers between devices: 67.9 us -> 0.02 us  [per_device(): lax.all_gather(own_keys, 'ctx', axis=0, tiled=True)]
  transfers between devices with their start and end apart: 11 -> 13, of which waited for: 10 -> 10; matrix products, arithmetic and copies ran while one was open for 8% -> 13% of each run, Pallas kernels for 0% -> 0%
where the time goes in v1:
time: 2810 us; the launch traced here: 2800 us
  waiting for transfers between devices  2300 us (82%)
  matrix products  253 us (9%)
  other arithmetic  181 us (6%)
  local copies, waits for them, and re-layouts  43.5 us (2%)
    ppermute x2, waiting for transfers between devices, per_device(): ppermute(weight_piece, 'wsh', [(nth, nth ^ mixed_arr) for nth in range(a_...  1570 us
    all_gather x1, waiting for transfers between devices, per_device(): lax.all_gather(attn_weight, 'wsh', axis=2, tiled=True)  197 us
    select_n x2, other arithmetic, per_device(): weight_piece = jnp.where(carry & mixed_arr == 0, after, piece_now)  146 us
    reduce_scatter x1, waiting for transfers between devices, per_device(): lax.psum_scatter(value_full, 'ctx', scatter_dimension=0, tiled=True)  133 us
    reduce_scatter x1, waiting for transfers between devices, per_device(): lax.psum_scatter(key_full, 'ctx', scatter_dimension=0, tiled=True)  123 us
    psum x1, waiting for transfers between devices, per_device(): model_grads, hidden_grads_out = lax.psum((shard_model, shard_hidden), 'ctx')  117 us
    reduce_scatter x1, waiting for transfers between devices, per_device(): lax.psum_scatter(spread_model, 'wsh', scatter_dimension=2, tiled=True)  56.9 us
  transfers between devices with their start and end apart: 13, of which 10 were waited for; matrix products, arithmetic and copies ran while one was open for 13% of the time, Pallas kernels for 0%

profile of v1, /device:TPU:0, one launch (start us, length us, event | category | flops | bytes accessed | tf_op | source)
XLA Modules:
  0.0 2804.1 jit_solution(10464396538050273572)
XLA Ops:
  7.9 11.5 copy.32
  20.4 6.4 all_gather.25
  30.2 9.2 all-gather.10.cloned.1.call-done
  39.4 4.7 fusion.23
  45.8 196.8 %all-gather.8.cloned.1.call-done = bf16[4,2048,2048]{1,2,0:T(8,128)(2,1)} async-done(((bf16[4,2048,512]{1,2,0:T(8,128)(2,1)}), bf16[4,2048,2048]{1,2,0:T(8,128)(2,1)}) %all-gather.8.cloned.1.call-update) | async-done | bytes 33554448 | tf_op jit(solution)/shard_map/all_gather | solution.py:116
  242.6 11.9 fusion.79
  257.7 2.7 copy.34
  260.4 2.5 copy.35
  272.7 37.2 %collective-permute-done = bf16[3,2048,2048]{2,1,0:T(8,128)(2,1)} collective-permute-done((bf16[3,2048,2048]{2,1,0:T(8,128)(2,1)}, bf16[3,2048,2048]{2,1,0:T(8,128)(2,1)}, u32[]{:S(2)}, u32[]{:S(2)}) %collective-permute-start) | collective-permute-done | bytes 25165856 | tf_op jit(solution)/shard_map/ppermute | solution.py:192
  309.9 49.8 %maximum_select_fusion.1 = bf16[3,2048,4096]{2,1,0:T(8,128)(2,1)} fusion(bf16[3,2048,2048]{2,1,0:T(8,128)(2,1)} %collective-permute-done, bf16[3,2048,2048]{2,1,0:T(8,128)(2,1)} %param.13, pred[]{:T(512)S(6)} %eq.19), kind=kLoop, calls=%fused_computation.1 | loop fusion | flops 226492416 | bytes 100663296 | tf_op jit(solution)/shard_map/jit(_where)/select_n | solution.py:195
  361.0 6.6 fusion.21
  368.5 4.3 fusion.18
  376.2 48.9 %all-gather.18.cloned.1.call-done = bf16[1,1024,2048]{1,2,0:T(8,128)(2,1)} async-done(((bf16[1,128,2048]{1,2,0:T(8,128)(2,1)}), bf16[1,1024,2048]{1,2,0:T(8,128)(2,1)}) %all-gather.18.cloned.1.call-update) | async-done | bytes 4194320 | tf_op jit(solution)/shard_map/all_gather | solution.py:142
  425.1 7.2 convolution_convert_fusion
  432.6 9.4 fusion.17
  444.0 3.9 convolution_multiply_fusion.1
  447.9 3.9 convolution_multiply_fusion
  451.8 1529.1 %collective-permute-done.1 = bf16[3,2048,4096]{2,1,0:T(8,128)(2,1)} collective-permute-done((bf16[3,2048,4096]{2,1,0:T(8,128)(2,1)}, bf16[3,2048,4096]{2,1,0:T(8,128)(2,1)}, u32[]{:S(2)}, u32[]{:S(2)}) %collective-permute-start.1) | collective-permute-done | bytes 50331680 | tf_op jit(solution)/shard_map/ppermute | solution.py:192
  1980.9 96.1 %maximum_select_fusion = bf16[3,2048,8192]{2,1,0:T(8,128)(2,1)} fusion(bf16[3,2048,4096]{2,1,0:T(8,128)(2,1)} %collective-permute-done.1, bf16[3,2048,4096]{2,1,0:T(8,128)(2,1)} %maximum_select_fusion.1, pred[]{:T(512)S(6)} %eq.18), kind=kLoop, calls=%fused_computation | loop fusion | flops 452984832 | bytes 201326592 | tf_op jit(solution)/shard_map/jit(_where)/select_n | solution.py:195
  2077.0 16.2 fusion.12
  2093.2 15.1 multiply_convert_fusion.4
  2110.7 19.3 fusion.59
  2131.9 15.0 fusion
  2146.9 4.9 convolution_add_fusion
  2151.8 16.2 fusion.11
  2168.0 18.7 multiply_convert_fusion.3
  2188.0 17.0 fusion.4
  2205.0 16.3 fusion.41
  2225.3 4.7 fusion.16
  2231.5 8.2 multiply_reduce_fusion
  2239.8 2.5 multiply_convert_fusion
  2242.3 4.7 broadcast_multiply_fusion
  2247.1 9.4 fusion.86
  2260.1 3.5 convolution_bitcast_fusion
  2263.6 3.4 bitcast_multiply_fusion
  2267.1 4.8 fusion.49
  2271.9 123.2 %reduce-scatter.5.cloned.1.call-done = f32[128,2048]{0,1:T(8,128)} async-done(((f32[1024,2048]{0,1:T(8,128)}), f32[128,2048]{0,1:T(8,128)}) %reduce-scatter.5.cloned.1.call-update) | async-done | bytes 1048592 | tf_op jit(solution)/shard_map/reduce_scatter | solution.py:319
  2402.2 2.7 copy.41
  2404.8 3.0 pad_maximum_fusion.3
  2407.8 2.5 copy.46
  2412.3 133.3 %reduce-scatter.7.cloned.1.call-done = f32[128,2048]{0,1:T(8,128)} async-done(((f32[1024,2048]{0,1:T(8,128)}), f32[128,2048]{0,1:T(8,128)}) %reduce-scatter.7.cloned.1.call-update) | async-done | bytes 1048592 | tf_op jit(solution)/shard_map/reduce_scatter | solution.py:320
  2552.5 3.3 bitcast_multiply_fusion.1
  2555.8 49.4 %reduce-scatter.11.cloned.1.call-done = f32[3,64,2048]{2,1,0:T(8,128)} async-done(((f32[3,64,8192]{2,1,0:T(8,128)}), f32[3,64,2048]{2,1,0:T(8,128)}) %reduce-scatter.11.cloned.1.call-update) | async-done | bytes 1572880 | tf_op jit(solution)/shard_map/reduce_scatter | solution.py:367
  2605.2 56.9 %reduce-scatter.9.cloned.1.call-done = f32[11,64,512]{2,1,0:T(8,128)} async-done(((f32[11,64,2048]{2,1,0:T(8,128)}), f32[11,64,512]{2,1,0:T(8,128)}) %reduce-scatter.9.cloned.1.call-update) | async-done | bytes 1441808 | tf_op jit(solution)/shard_map/reduce_scatter | solution.py:366
  2663.5 11.3 fusion.35
  2674.8 117.3 %all-reduce.3.cloned.1.call-done = (f32[11,64,512]{2,1,0:T(8,128)}, f32[3,64,2048]{2,1,0:T(8,128)}) async-done(((f32[11,64,512]{2,1,0:T(8,128)}, f32[3,64,2048]{2,1,0:T(8,128)}), (f32[11,64,512]{2,1,0:T(8,128)}, f32[3,64,2048]{2,1,0:T(8,128)})) %all-reduce.3.cloned.1.call-update) | async-done | bytes 3014672 | tf_op jit(solution)/shard_map/psum | solution.py:369
  2792.1 2.6 copy.86
  2794.7 2.7 copy.87
  (250 shorter events, 58.9 us)
Async XLA Ops:
  7.2 32.2 %all-gather.10.cloned.1.call-start = ((), (), s32[]{:S(2)}) async-start(), calls=%async_computation.5 | async-start | bytes 3604480 | tf_op jit(solution)/shard_map/all_gather | solution.py:118
  7.9 234.7 %all-gather.8.cloned.1.call-start = ((), (), s32[]{:S(2)}) async-start(), calls=%async_computation.4 | async-start | bytes 41943040 | tf_op jit(solution)/shard_map/all_gather | solution.py:116
  19.5 9.9 copy-start.72
  19.5 341.5 %all-gather.14.cloned.1.call-start = ((), (), s32[]{:S(2)}) async-start(), calls=%async_computation.7 | async-start | bytes 3932160 | tf_op jit(solution)/shard_map/all_gather | solution.py:197
  20.2 348.3 %all-gather.12.cloned.1.call-start = ((), (), s32[]{:S(2)}) async-start(), calls=%async_computation.6 | async-start | bytes 4718592 | tf_op jit(solution)/shard_map/all_gather | solution.py:141
  27.5 236.4 %copy-start.44 = (f32[1,2048]{1,0:T(1,128)}, f32[1,2048]{1,0:T(1,128)S(1)}, u32[]{:S(2)}) copy-start(f32[1,2048]{1,0:T(1,128)S(1)} %get-tuple-element.38) | copy-start | bytes 24580
  27.5 237.8 %copy-start.46 = (f32[1,2048]{1,0:T(1,128)}, f32[1,2048]{1,0:T(1,128)S(1)}, u32[]{:S(2)}) copy-start(f32[1,2048]{1,0:T(1,128)S(1)} %get-tuple-element.39) | copy-start | bytes 24580
  27.5 415.5 %copy-start.48 = (f32[1,2048]{1,0:T(1,128)}, f32[1,2048]{1,0:T(1,128)S(1)}, u32[]{:S(2)}) copy-start(f32[1,2048]{1,0:T(1,128)S(1)} %get-tuple-element.37) | copy-start | bytes 24580
  30.2 235.3 %copy-start.32 = (f32[128,64]{1,0:T(8,128)}, f32[128,64]{1,0:T(8,128)S(1)}, u32[]{:S(2)}) copy-start(f32[128,64]{1,0:T(8,128)S(1)} %get-tuple-element.40) | copy-start | bytes 98308
  30.2 235.3 %copy-start.34 = (f32[128,64]{1,0:T(8,128)}, f32[128,64]{1,0:T(8,128)S(1)}, u32[]{:S(2)}) copy-start(f32[128,64]{1,0:T(8,128)S(1)} %get-tuple-element.41) | copy-start | bytes 98308
  45.8 208.7 %copy-start.53 = (bf16[3,16,128]{2,1,0:T(8,128)(2,1)}, bf16[3,16,128]{2,1,0:T(8,128)(2,1)S(1)}, u32[]{:S(2)}) copy-start(bf16[3,16,128]{2,1,0:T(8,128)(2,1)S(1)} %convolution_convert_fusion.1) | copy-start | bytes 36868
  256.1 14.3 copy-start.1
  270.4 154.8 %all-gather.18.cloned.1.call-start = ((), (), s32[]{:S(2)}) async-start(), calls=%async_computation.13 | async-start | bytes 4718592 | tf_op jit(solution)/shard_map/all_gather | solution.py:142
  271.3 1860.7 %all-gather.16.cloned.1.call-start = ((), (), s32[]{:S(2)}) async-start(), calls=%async_computation.8 | async-start | bytes 125829120 | tf_op jit(solution)/shard_map/all_gather | solution.py:227
  271.9 2123.2 %reduce-scatter.5.cloned.1.call-start = ((), (), s32[]{:S(2)}) async-start(), calls=%async_computation.9 | async-start | bytes 9437184 | tf_op jit(solution)/shard_map/reduce_scatter | solution.py:319
  272.4 37.6 %collective-permute-start = (bf16[3,2048,2048]{2,1,0:T(8,128)(2,1)}, bf16[3,2048,2048]{2,1,0:T(8,128)(2,1)}, u32[]{:S(2)}, u32[]{:S(2)}) collective-permute-start(bf16[3,2048,2048]{2,1,0:T(8,128)(2,1)} %param.13), channel_id=1, source_target_pairs={{0,1},{1,0},{2,3},{3,2},{4,5},{5,4},{6,7},{7,6},{8,9},{9,8},{10,11... | collective-permute-start | bytes 75497480 | tf_op jit(solution)/shard_map/ppermute | solution.py:192
  359.8 1621.1 %collective-permute-start.1 = (bf16[3,2048,4096]{2,1,0:T(8,128)(2,1)}, bf16[3,2048,4096]{2,1,0:T(8,128)(2,1)}, u32[]{:S(2)}, u32[]{:S(2)}) collective-permute-start(bf16[3,2048,4096]{2,1,0:T(8,128)(2,1)} %maximum_select_fusion.1), channel_id=1, source_target_pairs={{0,2},{1,3},{2,0},{3,1},{4,6},{5,7},{6,4},{7,5},{8,10},{9,11},{10,... | collective-permute-start | bytes 150994944 | tf_op jit(solution)/shard_map/ppermute | solution.py:192
  360.9 64.2 %copy-start.13 = (pred[128,1024]{1,0:T(8,128)(4,1)}, pred[128,1024]{1,0:T(8,128)(4,1)S(1)}, u32[]{:S(2)}) copy-start(pred[128,1024]{1,0:T(8,128)(4,1)S(1)} %compare_and_fusion) | copy-start | bytes 393220
  376.2 56.1 %copy-start.42 = (f32[16,128]{1,0:T(8,128)}, f32[16,128]{1,0:T(8,128)S(1)}, u32[]{:S(2)}) copy-start(f32[16,128]{1,0:T(8,128)S(1)} %log_add_fusion) | copy-start | bytes 24580
  432.3 9.6 copy-start.29
  432.5 9.4 copy-start.55
  432.5 10.9 copy-start.7
  442.3 9.4 copy-start.4
  443.7 1724.3 %copy-start.15 = (bf16[128,2048]{1,0:T(8,128)(2,1)}, bf16[128,2048]{1,0:T(8,128)(2,1)S(1)}, u32[]{:S(2)}) copy-start(bf16[128,2048]{1,0:T(8,128)(2,1)S(1)} %fusion.73) | copy-start | bytes 1572868
  2093.2 17.5 copy-start.52
  2093.2 17.5 copy-start.66
  2110.3 19.6 copy-start.57
  2131.7 15.2 copy-start.17
  2205.0 16.4 copy-start.5
  2205.0 16.4 copy-start.49
  2205.0 17.7 copy-start.8
  2205.0 17.7 copy-start.26
  2205.0 17.8 copy-start.65
  2205.0 17.8 copy-start.69
  2247.0 298.6 %reduce-scatter.7.cloned.1.call-start = ((), (), s32[]{:S(2)}) async-start(), calls=%async_computation.10 | async-start | bytes 9437184 | tf_op jit(solution)/shard_map/reduce_scatter | solution.py:320
  2256.5 348.7 %reduce-scatter.11.cloned.1.call-start = ((), (), s32[]{:S(2)}) async-start(), calls=%async_computation.12 | async-start | bytes 7864320 | tf_op jit(solution)/shard_map/reduce_scatter | solution.py:367
  2267.0 395.2 %reduce-scatter.9.cloned.1.call-start = ((), (), s32[]{:S(2)}) async-start(), calls=%async_computation.11 | async-start | bytes 7208960 | tf_op jit(solution)/shard_map/reduce_scatter | solution.py:366
  2271.8 127.0 %copy-start.33 = (f32[128,64]{1,0:T(8,128)S(1)}, f32[128,64]{1,0:T(8,128)}, u32[]{:S(2)}) copy-start(f32[128,64]{1,0:T(8,128)} %copy-done.32) | copy-start | bytes 98308
  2271.8 127.0 %copy-start.35 = (f32[128,64]{1,0:T(8,128)S(1)}, f32[128,64]{1,0:T(8,128)}, u32[]{:S(2)}) copy-start(f32[128,64]{1,0:T(8,128)} %copy-done.34) | copy-start | bytes 98308
  2407.8 139.1 %copy-start.60 = (f32[128]{0:T(128)S(1)}, f32[128]{0:T(128)}, u32[]{:S(2)}) copy-start(f32[128]{0:T(128)} %copy-done.59) | copy-start | bytes 1540
  2407.8 139.1 %copy-start.62 = (f32[128]{0:T(128)S(1)}, f32[128]{0:T(128)}, u32[]{:S(2)}) copy-start(f32[128]{0:T(128)} %copy-done.61) | copy-start | bytes 1540
  2407.8 139.1 %copy-start.67 = (f32[128]{0:T(128)S(1)}, f32[128]{0:T(128)}, u32[]{:S(2)}) copy-start(f32[128]{0:T(128)} %get-tuple-element.44) | copy-start | bytes 1540
  2407.8 139.1 %copy-start.68 = (f32[128]{0:T(128)S(1)}, f32[128]{0:T(128)}, u32[]{:S(2)}) copy-start(f32[128]{0:T(128)} %get-tuple-element.61) | copy-start | bytes 1540
  2555.8 107.7 %copy-start.28 = (f32[128,2048]{1,0:T(8,128)S(1)}, f32[128,2048]{1,0:T(8,128)}, u32[]{:S(2)}) copy-start(f32[128,2048]{1,0:T(8,128)} %copy-done.27) | copy-start | bytes 3145732
  2555.8 107.7 %copy-start.37 = (bf16[1,128,2048]{1,2,0:T(8,128)(2,1)S(1)}, bf16[1,128,2048]{1,2,0:T(8,128)(2,1)}, u32[]{:S(2)}) copy-start(bf16[1,128,2048]{1,2,0:T(8,128)(2,1)} %copy-done.36) | copy-start | bytes 1572868
  2555.8 107.7 %copy-start.39 = (bf16[1,128,2048]{1,2,0:T(8,128)(2,1)S(1)}, bf16[1,128,2048]{1,2,0:T(8,128)(2,1)}, u32[]{:S(2)}) copy-start(bf16[1,128,2048]{1,2,0:T(8,128)(2,1)} %copy-done.38) | copy-start | bytes 1572868
  2555.8 107.7 %copy-start.41 = (bf16[1,128,2048]{1,2,0:T(8,128)(2,1)S(1)}, bf16[1,128,2048]{1,2,0:T(8,128)(2,1)}, u32[]{:S(2)}) copy-start(bf16[1,128,2048]{1,2,0:T(8,128)(2,1)} %copy-done.40) | copy-start | bytes 1572868
  2555.8 236.4 %all-reduce.3.cloned.1.call-start = ((), (), s32[]{:S(2)}) async-start(), calls=%async_computation.14 | async-start | bytes 6029312 | tf_op jit(solution)/shard_map/psum | solution.py:369
  (41 other events, 170.6 us)
Sparse Core Ops, SparseCore 0:
  9.5 29.8 all-gather.9
  41.0 201.5 all-gather.7
  244.1 28.4 all-gather.13
  275.2 74.6 all-gather.11
  352.3 72.7 all-gather.17
  426.6 1121.4 all-gather.15
  2247.2 147.8 reduce-scatter.4
  2398.6 146.9 reduce-scatter.6
  2548.2 57.0 reduce-scatter.10
  2607.6 54.5 reduce-scatter.8
  2666.0 126.1 all-reduce.2
